TPU v7x, 32 devices: a whole 2x2x4 slice. The times are simulated.
32 devices in a mesh: dp: 2 (over y), fsdp: 16 (over z, x, core).
Axes of the slice: x: 2, y: 2, z: 4, core: 2. Of those that a mesh axis runs over, the one named last changes fastest.
Arguments:
- tokens: bfloat16 [64, 512, 768], P(('dp', 'fsdp')), may hold values from -6 to 6
- out_grad: bfloat16 [64, 512, 768], P(('dp', 'fsdp')), may hold values from -6 to 6
- lengths: int32 [64], P(('dp', 'fsdp')), may hold values from 128 to 512, as said below
- labels: int32 [64], P(('dp', 'fsdp')), may hold values from 0 to 2
- exit_layers: int32 [64], P(('dp', 'fsdp')), may hold values from 0 to 11, as said below
- mat_master: float32 [9984, 768], P('fsdp')
- mat_first: float32 [9984, 768], P('fsdp')
- mat_second: float32 [9984, 768], P('fsdp'), as said below
- vec_master: float32 [16, 768], P(None, 'fsdp')
- vec_first: float32 [16, 768], P(None, 'fsdp')
- vec_second: float32 [16, 768], P(None, 'fsdp'), as said below
- cls_bias: float32 [3], replicated, may hold values from -3 to 3
- cls_first: float32 [3], replicated
- cls_second: float32 [3], replicated, as said below
Outputs:
- block_out: bfloat16 [64, 512, 768], P(('dp', 'fsdp'))
- input_grad: bfloat16 [64, 512, 768], P(('dp', 'fsdp'))
- ramp_loss: float32 [], replicated
- mat_master_new: float32 [9984, 768], P('fsdp')
- mat_first_new: float32 [9984, 768], P('fsdp')
- mat_second_new: float32 [9984, 768], P('fsdp')
- mat_copy: bfloat16 [9984, 768], P('fsdp')
- vec_master_new: float32 [16, 768], P(None, 'fsdp')
- vec_first_new: float32 [16, 768], P(None, 'fsdp')
- vec_second_new: float32 [16, 768], P(None, 'fsdp')
- vec_copy: bfloat16 [16, 768], P(None, 'fsdp')
- cls_bias_new: float32 [3], replicated
- cls_first_new: float32 [3], replicated
- cls_second_new: float32 [3], replicated
Inputs may be any that keep to these rules, and one draw needn't show every extreme that they name: Keys at positions of lengths or later are padding; some sequence has 512 tokens and some 512 // 4. `exit_layers`: a sequence whose exit layer is below 6 has left the encoder and is out of the loss; some sequence exits at layer 0 and some at the last. `mat_second`: positive. `vec_second`: positive. `cls_second`: positive.
All inputs are finite; a program needn't handle non-finite values.
Results may differ from a plain program's by a relative error of at most 0.02.
Values may be sent and summed in bfloat16 or wider, within the bound.
No kernel may reach another device: no remote copies, remote signals or barrier semaphores. Data moves between devices by JAX's collectives and lax.ppermute only.
A program may use at most 192 MiB of HBM per device.

v0:
```python
import jax
import jax.numpy as jnp
from jax import lax
from jax.sharding import PartitionSpec as P

D = 768
H = 12
HD = 64
FF = 3072
LAYER = 6
NCLS = 3
L = 512
STEP = 10
BETA_ONE = 0.9
BETA_TWO = 0.999
ADAM_EPS = 1e-08
WEIGHT_DECAY = 0.01
LN_EPS = 1e-12
VEC_RATE = 0.5
MASK_FILL = -1000000000.0


def product(first_arg, second_arg):
    return jnp.dot(first_arg, second_arg, preferred_element_type=jnp.float32)


def product_last(first_arg, second_arg):
    return lax.dot_general(
        first_arg, second_arg, (((1,), (1,)), ((), ())), preferred_element_type=jnp.float32
    )


def product_first(first_arg, second_arg):
    return lax.dot_general(
        first_arg, second_arg, (((0,), (0,)), ((), ())), preferred_element_type=jnp.float32
    )


def norm_forward(hidden, gain_vec, shift_vec):
    centre = jnp.mean(hidden, axis=-1, keepdims=True)
    centred = hidden - centre
    spread = jnp.mean(centred * centred, axis=-1, keepdims=True)
    inv_dev = lax.rsqrt(spread + LN_EPS)
    normed = centred * inv_dev
    return (normed * gain_vec + shift_vec, normed, inv_dev)


def norm_backward(grad_in, normed, inv_dev, gain_vec):
    scaled = grad_in * gain_vec
    return inv_dev * (
        scaled
        - jnp.mean(scaled, axis=-1, keepdims=True)
        - normed * jnp.mean(scaled * normed, axis=-1, keepdims=True)
    )


def split_matrices(matrices):
    return (
        matrices[0:D],
        matrices[D : 2 * D],
        matrices[2 * D : 3 * D],
        matrices[3 * D : 4 * D],
        matrices[4 * D : 5 * D],
        matrices[5 * D : 5 * D + FF],
        matrices[5 * D + FF : 5 * D + 2 * FF],
    )


def split_vectors(vectors):
    inner_rows = FF // D
    values_f = vectors.astype(jnp.float32)
    return (
        values_f[0],
        values_f[1],
        values_f[2],
        values_f[3],
        values_f[4],
        values_f[5],
        values_f[6],
        values_f[7],
        values_f[8],
        values_f[9 : 9 + inner_rows].reshape(FF),
        vectors[9 + inner_rows : 9 + inner_rows + NCLS],
    )


def row_rates(row_index):
    base_rate = D ** (-0.5)
    return jnp.where(
        (row_index >= 3 * D) & (row_index < 4 * D),
        8.0 * base_rate,
        jnp.where(row_index >= 5 * D + FF, 1.5 * FF ** (-0.5), base_rate),
    )


def adam_update(master, first_mom, second_mom, grad_in, rate, decay):
    first_new = BETA_ONE * first_mom + (1.0 - BETA_ONE) * grad_in
    second_new = BETA_TWO * second_mom + (1.0 - BETA_TWO) * grad_in * grad_in
    fix_one = 1.0 - BETA_ONE**STEP
    fix_two = 1.0 - BETA_TWO**STEP
    direction = first_new / fix_one / (jnp.sqrt(second_new / fix_two) + ADAM_EPS)
    master_new = master - rate * (direction + decay * master)
    return (master_new, first_new, second_new)


def masked_scores(q_seq, k_seq, length):
    score_scale = HD ** (-0.5)
    scores = (
        jnp.einsum("qhd,khd->hqk", q_seq, k_seq, preferred_element_type=jnp.float32) * score_scale
    )
    key_valid = jnp.arange(q_seq.shape[0]) < length
    return jnp.where(key_valid[None, None, :], scores, MASK_FILL)


def attend(seq_parts):
    q_seq, k_seq, v_seq, length = seq_parts
    scores = masked_scores(q_seq, k_seq, length)
    row_max = jnp.max(scores, axis=-1, keepdims=True)
    exp_scores = jnp.exp(scores - row_max)
    exp_total = jnp.sum(exp_scores, axis=-1, keepdims=True)
    attn_probs = exp_scores / exp_total
    log_total = row_max + jnp.log(exp_total)
    context = jnp.einsum(
        "hqk,khd->qhd", attn_probs.astype(jnp.bfloat16), v_seq, preferred_element_type=jnp.float32
    )
    return (context.astype(jnp.bfloat16), log_total)


def attend_back(seq_parts):
    q_seq, k_seq, v_seq, length, log_total, grad_ctx = seq_parts
    score_scale = HD ** (-0.5)
    attn_probs = jnp.exp(masked_scores(q_seq, k_seq, length) - log_total)
    grad_probs = jnp.einsum("qhd,khd->hqk", grad_ctx, v_seq, preferred_element_type=jnp.float32)
    grad_values = jnp.einsum(
        "hqk,qhd->khd",
        attn_probs.astype(jnp.bfloat16),
        grad_ctx,
        preferred_element_type=jnp.float32,
    )
    grad_scores = attn_probs * (
        grad_probs - jnp.sum(attn_probs * grad_probs, axis=-1, keepdims=True)
    )
    rounded = grad_scores.astype(jnp.bfloat16)
    grad_query = (
        jnp.einsum("hqk,khd->qhd", rounded, k_seq, preferred_element_type=jnp.float32) * score_scale
    )
    grad_keys = (
        jnp.einsum("hqk,qhd->khd", rounded, q_seq, preferred_element_type=jnp.float32) * score_scale
    )
    return (
        grad_query.astype(jnp.bfloat16),
        grad_keys.astype(jnp.bfloat16),
        grad_values.astype(jnp.bfloat16),
    )


def on_device(
    tokens,
    out_grad,
    lengths,
    labels,
    exit_layers,
    mat_master,
    mat_first,
    mat_second,
    vec_master,
    vec_first,
    vec_second,
    cls_bias,
    cls_first,
    cls_second,
):
    seq_count = tokens.shape[0]
    tok_count = seq_count * L
    active = (exit_layers >= LAYER).astype(jnp.float32)
    mat_low = mat_master.astype(jnp.bfloat16)
    vec_low = vec_master.astype(jnp.bfloat16)
    matrices, vectors = (
        lax.all_gather(mat_low, "fsdp", axis=0, tiled=True),
        lax.all_gather(vec_low, "fsdp", axis=1, tiled=True),
    )
    w_query, w_key, w_value, w_out, w_pool, w_inner, w_outer = split_matrices(matrices)
    (
        b_query,
        b_value,
        b_out,
        gain_one,
        shift_one,
        b_outer,
        gain_two,
        shift_two,
        b_pool,
        b_inner,
        w_class,
    ) = split_vectors(vectors)
    token_rows = tokens.reshape(tok_count, D)
    query_rows = (product(token_rows, w_query) + b_query).astype(jnp.bfloat16)
    key_rows = product(token_rows, w_key).astype(jnp.bfloat16)
    value_rows = (product(token_rows, w_value) + b_value).astype(jnp.bfloat16)
    q_heads = query_rows.reshape(seq_count, L, H, HD)
    k_heads = key_rows.reshape(seq_count, L, H, HD)
    v_heads = value_rows.reshape(seq_count, L, H, HD)
    context, log_total = lax.map(attend, (q_heads, k_heads, v_heads, lengths))
    ctx_rows = context.reshape(tok_count, D)
    resid_attn = token_rows.astype(jnp.float32) + (product(ctx_rows, w_out) + b_out)
    normed_out, normed_one, inv_one = norm_forward(resid_attn, gain_one, shift_one)
    normed_low = normed_out.astype(jnp.bfloat16)
    inner_pre = product_last(normed_low, w_inner) + b_inner
    activated = jax.nn.gelu(inner_pre, approximate=False).astype(jnp.bfloat16)
    resid_ffn = normed_out + (product(activated, w_outer) + b_outer)
    layer_out, normed_two, inv_two = norm_forward(resid_ffn, gain_two, shift_two)
    block_out = layer_out.astype(jnp.bfloat16).reshape(seq_count, L, D)
    first_row = block_out[:, 0, :]
    pooled = jnp.tanh(product(first_row, w_pool) + b_pool)
    pooled_low = pooled.astype(jnp.bfloat16)
    logits = product_last(pooled_low, w_class) + cls_bias
    log_norm = jax.nn.logsumexp(logits, axis=-1)
    onehot = (labels[:, None] == jnp.arange(NCLS)[None, :]).astype(jnp.float32)
    cross_ent = log_norm - jnp.sum(logits * onehot, axis=-1)
    ce_sum = jnp.sum(active * cross_ent)
    class_error = active[:, None] * (jnp.exp(logits - log_norm[:, None]) - onehot)
    error_sum = jnp.sum(class_error, axis=0)
    ce_total, active_count, error_total = lax.psum(
        (ce_sum, jnp.sum(active), error_sum), ("dp", "fsdp")
    )
    matrices, vectors = (
        lax.all_gather(mat_low, "fsdp", axis=0, tiled=True),
        lax.all_gather(vec_low, "fsdp", axis=1, tiled=True),
    )
    w_query, w_key, w_value, w_out, w_pool, w_inner, w_outer = split_matrices(matrices)
    (
        b_query,
        b_value,
        b_out,
        gain_one,
        shift_one,
        b_outer,
        gain_two,
        shift_two,
        b_pool,
        b_inner,
        w_class,
    ) = split_vectors(vectors)
    grad_logit = (class_error / active_count).astype(jnp.bfloat16)
    grad_pool = product(grad_logit, w_class)
    grad_pre = (grad_pool * (1.0 - pooled * pooled)).astype(jnp.bfloat16)
    grad_b_pool = jnp.sum(grad_pre.astype(jnp.float32), axis=0)
    grad_w_pool = product_first(first_row, grad_pre)
    grad_w_class = product_first(grad_logit, pooled_low)
    grad_first = product_last(grad_pre, w_pool)
    grad_layer = out_grad.astype(jnp.float32).at[:, 0, :].add(grad_first).reshape(tok_count, D)
    grad_gain_two = jnp.sum(grad_layer * normed_two, axis=0)
    grad_shift_two = jnp.sum(grad_layer, axis=0)
    grad_resid_ffn = norm_backward(grad_layer, normed_two, inv_two, gain_two)
    grad_ffn = grad_resid_ffn.astype(jnp.bfloat16)
    grad_b_outer = jnp.sum(grad_ffn.astype(jnp.float32), axis=0)
    inner_again = product_last(normed_low, w_inner) + b_inner
    gelu_out, gelu_pull = jax.vjp(
        lambda inner_val: jax.nn.gelu(inner_val, approximate=False), inner_again
    )
    activ_again = gelu_out.astype(jnp.bfloat16)
    grad_w_outer = product_first(activ_again, grad_ffn)
    grad_activ = product_last(grad_ffn, w_outer)
    grad_inner = gelu_pull(grad_activ)[0].astype(jnp.bfloat16)
    grad_b_inner = jnp.sum(grad_inner.astype(jnp.float32), axis=0)
    grad_w_inner = product_first(grad_inner, normed_low)
    grad_normed = grad_resid_ffn + product(grad_inner, w_inner)
    grad_gain_one = jnp.sum(grad_normed * normed_one, axis=0)
    grad_shift_one = jnp.sum(grad_normed, axis=0)
    grad_resid_attn = norm_backward(grad_normed, normed_one, inv_one, gain_one)
    grad_attn = grad_resid_attn.astype(jnp.bfloat16)
    grad_b_out = jnp.sum(grad_attn.astype(jnp.float32), axis=0)
    grad_w_out = product_first(ctx_rows, grad_attn)
    grad_ctx = product_last(grad_attn, w_out).astype(jnp.bfloat16).reshape(seq_count, L, H, HD)
    grad_q, grad_k, grad_v = lax.map(
        attend_back, (q_heads, k_heads, v_heads, lengths, log_total, grad_ctx)
    )
    grad_q = grad_q.reshape(tok_count, D)
    grad_k = grad_k.reshape(tok_count, D)
    grad_v = grad_v.reshape(tok_count, D)
    grad_b_query = jnp.sum(grad_q.astype(jnp.float32), axis=0)
    grad_b_value = jnp.sum(grad_v.astype(jnp.float32), axis=0)
    grad_w_query = product_first(token_rows, grad_q)
    grad_w_key = product_first(token_rows, grad_k)
    grad_w_value = product_first(token_rows, grad_v)
    grad_tokens = (
        grad_resid_attn
        + product_last(grad_q, w_query)
        + product_last(grad_k, w_key)
        + product_last(grad_v, w_value)
    )
    input_grad = grad_tokens.astype(jnp.bfloat16).reshape(seq_count, L, D)
    mat_grad = jnp.concatenate(
        [
            grad_w_query,
            grad_w_key,
            grad_w_value,
            grad_w_out,
            grad_w_pool,
            grad_w_inner,
            grad_w_outer,
        ],
        axis=0,
    )
    head_rows = jnp.stack(
        [
            grad_b_query,
            grad_b_value,
            grad_b_out,
            grad_gain_one,
            grad_shift_one,
            grad_b_outer,
            grad_gain_two,
            grad_shift_two,
            grad_b_pool,
        ],
        axis=0,
    )
    vec_grad = jnp.concatenate([head_rows, grad_b_inner.reshape(FF // D, D), grad_w_class], axis=0)
    mat_part, vec_part = (
        lax.psum_scatter(
            mat_grad.astype(jnp.bfloat16), "fsdp", scatter_dimension=0, tiled=True
        ).astype(jnp.float32),
        lax.psum_scatter(
            vec_grad.astype(jnp.bfloat16), "fsdp", scatter_dimension=1, tiled=True
        ).astype(jnp.float32),
    )
    mat_total, vec_total = (
        lax.psum(mat_part.astype(jnp.bfloat16), "dp").astype(jnp.float32),
        lax.psum(vec_part.astype(jnp.bfloat16), "dp").astype(jnp.float32),
    )
    ramp_loss = ce_total / active_count
    cls_grad = error_total / active_count
    shard_rows = mat_master.shape[0]
    row_index = lax.axis_index("fsdp") * shard_rows + jnp.arange(shard_rows)
    rates = row_rates(row_index)[:, None]
    mat_new, mat_first_new, mat_second_new = adam_update(
        mat_master, mat_first, mat_second, mat_total, rates, WEIGHT_DECAY
    )
    vec_new, vec_first_new, vec_second_new = adam_update(
        vec_master, vec_first, vec_second, vec_total, VEC_RATE, 0.0
    )
    cls_new, cls_first_new, cls_second_new = adam_update(
        cls_bias, cls_first, cls_second, cls_grad, VEC_RATE, 0.0
    )
    return (
        block_out,
        input_grad,
        ramp_loss,
        mat_new,
        mat_first_new,
        mat_second_new,
        mat_new.astype(jnp.bfloat16),
        vec_new,
        vec_first_new,
        vec_second_new,
        vec_new.astype(jnp.bfloat16),
        cls_new,
        cls_first_new,
        cls_second_new,
    )


def solution(mesh):
    placed = (
        P(("dp", "fsdp"), None, None),
        P(("dp", "fsdp"), None, None),
        P(("dp", "fsdp")),
        P(("dp", "fsdp")),
        P(("dp", "fsdp")),
        P("fsdp", None),
        P("fsdp", None),
        P("fsdp", None),
        P(None, "fsdp"),
        P(None, "fsdp"),
        P(None, "fsdp"),
        P(),
        P(),
        P(),
    )
    return jax.shard_map(
        on_device,
        mesh=mesh,
        in_specs=placed,
        out_specs=(
            P(("dp", "fsdp"), None, None),
            P(("dp", "fsdp"), None, None),
            P(),
            P("fsdp", None),
            P("fsdp", None),
            P("fsdp", None),
            P("fsdp", None),
            P(None, "fsdp"),
            P(None, "fsdp"),
            P(None, "fsdp"),
            P(None, "fsdp"),
            P(),
            P(),
            P(),
        ),
        check_vma=False,
    )
```

profile of v0, /device:TPU:0, one launch (start us, length us, event | category | flops | bytes accessed | tf_op | source)
XLA Modules:
  0.0 690.1 jit_solution(1368104361643564995)
XLA Ops:
  10.0 23.6 %all-gather = bf16[16,48,16]{1,2,0:T(8,128)(2,1)S(1)} all-gather(bf16[1,48,16]{1,2,0:T(8,128)(2,1)S(1)} %convert_bitcast_fusion), channel_id=1, replica_groups=mesh['dp'=2,'fsdp'=16] {'fsdp'}, dimensions={0}, use_global_device_ids=true | all-gather | bytes 26112 | tf_op jit(solution)/shard_map/all_gather | solution.py:180
  38.3 93.3 %all-gather.3.cloned.1.call-done = bf16[9984,768]{1,0:T(8,128)(2,1)} async-done(((bf16[624,768]{1,0:T(8,128)(2,1)}), bf16[9984,768]{1,0:T(8,128)(2,1)}) %all-gather.3.cloned.1.call-update) | async-done | bytes 15335440 | tf_op jit(solution)/shard_map/all_gather | solution.py:179
  155.4 22.9 %while.27 = (s32[]{:T(128)}, bf16[2,512,12,64]{1,3,2,0:T(8,128)(2,1)}, f32[2,12,512,1]{2,1,3,0:T(8,128)S(1)}, bf16[2,512,12,64]{1,3,2,0:T(8,128)(2,1)}, s32[2]{0...) while((s32[]{:T(128)}, ...), condition=%wide.region_3.4_spmd, body=%wide.region_0.3_spmd.sunk | while | flops 843442688 | bytes 47427716 | solution.py:203
  187.1 36.7 %multiply_convert_fusion.3 = (bf16[1024,3072]{1,0:T(8,128)(2,1)S(1)}, f32[1024,3072]{1,0:T(8,128)}, f32[1024,3072]{1,0:T(8,128)}) fusion(f32[3072]{0:T(1024)S(1)} %add.241, bf16[9984,768]{1,0:T(8,128)(2,1)} %all-gather.3.cloned.1.call-done, f32[1024,768]{1,0:T(8,128)S(1)} %get-tuple-element.291, f32[768]{0:T(1024)S(1)} %get-tuple-element.220, ...), kind=kOutput, calls=%fused_computation.65 | convolution fusion | flops 5043388416 | bytes 39348224 | tf_op jit(solution)/shard_map/dot_general | solution.py:28
  223.9 9.9 %fusion.139 = (f32[1024]{0:T(1024)S(1)}, f32[1024,768]{1,0:T(8,128)S(1)}) fusion(f32[768]{0:T(1024)S(1)} %copy-done.61, bf16[1024,3072]{1,0:T(8,128)(2,1)S(1)} %get-tuple-element.284, bf16[9984,768]{1,0:T(8,128)(2,1)} %all-gather.3.cloned.1.call-done, f32[768]{0:T(1024)S(1)} %get-tuple-element.220, f32[768]{0:T(1024)S(1)} %get-tuple-element.221, ...), kind=kOutput, calls=%fused_computation.220 | convolution fusion | flops 4837342208 | bytes 17323008 | tf_op jit(solution)/shard_map/dot_general | solution.py:24
  239.0 39.1 %all-reduce = (f32[]{:T(128)}, f32[]{:T(128)}, f32[3]{0:T(128)}) all-reduce(f32[]{:T(128)} %get-tuple-element.228, f32[]{:T(128)} %get-tuple-element.227, f32[3]{0:T(128)S(1)} %get-tuple-element.281), channel_id=1, replica_groups=mesh['dp'=2,'fsdp'=16] {'dp','fsdp'}, use_global_device_ids=true, to_apply=%region_11.12 | all-reduce | flops 5 | bytes 40 | tf_op jit(solution)/shard_map/psum | solution.py:223
  289.1 4.3 convert_reduce_fusion.1
  293.4 19.4 %fusion.142 = (bf16[3072]{0:T(1024)(128)(2,1)}, bf16[1024,3072]{1,0:T(8,128)(2,1)}) fusion(f32[1024,3072]{1,0:T(8,128)} %get-tuple-element.285, bf16[9984,768]{1,0:T(8,128)(2,1)} %all-gather.3.cloned.1.call-done, f32[1024,768]{1,0:T(8,128)} %get-tuple-element.274, f32[1024,3072]{1,0:T(8,128)} %get-tuple-element.292, f32[3072]{0:T(1024)S(1)} %add.241), kind=kOutput, calls=%fused_computation.223 | convolution fusion | flops 4882953216 | bytes 39340032 | tf_op jit(solution)/shard_map/dot_general | solution.py:28
  312.8 10.5 %multiply_reduce_fusion.1 = (bf16[768]{0:T(1024)(128)(2,1)}, f32[1024]{0:T(1024)S(1)}, f32[1024]{0:T(1024)S(1)}, bf16[768]{0:T(1024)(128)(2,1)}, f32[1024,768]{1,0:T(8,128)S(1)}) fusion(f32[1024,768]{1,0:T(8,128)S(1)} %copy-done.14, f32[1024]{0:T(1024)S(1)} %add_rsqrt_fusion.1, f32[1024]{0:T(1024)S(1)} %broadcast_multiply_fusion.5, ...), kind=kOutput, calls=%fused_computation.93 | convolution fusion | flops 4839698432 | bytes 20469760 | tf_op jit(solution)/shard_map/dot_general | solution.py:24
  336.9 52.1 %while.28 = (s32[]{:T(128)}, bf16[2,512,12,64]{1,3,2,0:T(8,128)(2,1)}, bf16[2,512,12,64]{1,3,2,0:T(8,128)(2,1)}, bf16[2,512,12,64]{1,3,2,0:T(8,128)(2,1)}, bf16[...) while((s32[]{:T(128)}, ...), condition=%wide.region_18.19_spmd, body=%wide.region_16.18_spmd.sunk | while | flops 2062412288 | bytes 140180784 | solution.py:275
  340.0 7.3 %multiply_reduce_fusion.9 = (f32[12,512]{1,0:T(8,128)S(1)}, f32[12,512,512]{1,2,0:T(8,128)}) fusion(f32[12,512,512]{1,2,0:T(8,128)S(1)} %fusion.193, f32[12,512]{1,0:T(8,128)S(1)} %dynamic-slice_bitcast_fusion.2, pred[512]{0:T(512)(128)(4,1)S(1)} %iota_compare_fusion.6, bf16[2,512,12,64]{1,3,2,0:T(8,128)(2,1)S(1)} %copy-done.7, ...), kind=kOutput, calls=%fused_computation.23.clone.1 | convolution fusion | flops 418375680 | bytes 26797568 | tf_op jit(solution)/shard_map/while/body/eval_jaxpr/qhd,khd->hqk/dot_general | solution.py:133
  347.4 7.2 %multiply_convert_fusion.5 = bf16[12,512,512]{1,2,0:T(8,128)(2,1)S(1)} fusion(f32[12,512,512]{1,2,0:T(8,128)} %get-tuple-element.414, f32[12,512,512]{1,2,0:T(8,128)S(1)} %fusion.193, f32[12,512]{1,0:T(8,128)S(1)} %get-tuple-element.415, f32[12,512]{1,0:T(8,128)S(1)} %dynamic-slice_bitcast_fusion.2, pred[512]{0:T(512)(128)(4,1)S(1)} %iota_compare_fusion.6), kind=kLoop, calls=%fused_computation.22.clone.1 | loop fusion | flops 18874368 | bytes 31506944 | tf_op jit(solution)/shard_map/while/body/eval_jaxpr/convert_element_type | solution.py:143
  365.9 7.3 %multiply_reduce_fusion.9 = (f32[12,512]{1,0:T(8,128)S(1)}, f32[12,512,512]{1,2,0:T(8,128)}) fusion(f32[12,512,512]{1,2,0:T(8,128)S(1)} %fusion.193, f32[12,512]{1,0:T(8,128)S(1)} %dynamic-slice_bitcast_fusion.2, pred[512]{0:T(512)(128)(4,1)S(1)} %iota_compare_fusion.6, bf16[2,512,12,64]{1,3,2,0:T(8,128)(2,1)S(1)} %copy-done.7, ...), kind=kOutput, calls=%fused_computation.23.clone.1 | convolution fusion | flops 418375680 | bytes 26797568 | tf_op jit(solution)/shard_map/while/body/eval_jaxpr/qhd,khd->hqk/dot_general | solution.py:133
  373.2 7.2 %multiply_convert_fusion.5 = bf16[12,512,512]{1,2,0:T(8,128)(2,1)S(1)} fusion(f32[12,512,512]{1,2,0:T(8,128)} %get-tuple-element.414, f32[12,512,512]{1,2,0:T(8,128)S(1)} %fusion.193, f32[12,512]{1,0:T(8,128)S(1)} %get-tuple-element.415, f32[12,512]{1,0:T(8,128)S(1)} %dynamic-slice_bitcast_fusion.2, pred[512]{0:T(512)(128)(4,1)S(1)} %iota_compare_fusion.6), kind=kLoop, calls=%fused_computation.22.clone.1 | loop fusion | flops 18874368 | bytes 31506944 | tf_op jit(solution)/shard_map/while/body/eval_jaxpr/convert_element_type | solution.py:143
  408.5 7.8 %fusion.64 = bf16[9984,768]{1,0:T(8,128)(2,1)} fusion(bf16[9984,768]{1,0:T(8,128)(2,1)} %fusion.81, bf16[1024,3072]{1,0:T(8,128)(2,1)S(1)} %bitcast.232, f32[1024,768]{1,0:T(8,128)S(1)} %copy-done.15, f32[768]{0:T(1024)S(1)} %copy-done.60, f32[768]{0:T(1024)S(1)} %copy-done.43, f32[1024]{0:T(1024)S(1)} %copy-done.45, f32[1024]{0:T(1024)S(1)} %copy-done.37), kind=kOutput, calls=%fused_computation.82 | convolution fusion | flops 4838129664 | bytes 14170112 | tf_op jit(solution)/shard_map/dot_general | solution.py:34
  416.4 7.1 %fusion.63 = bf16[9984,768]{1,0:T(8,128)(2,1)} fusion(bf16[9984,768]{1,0:T(8,128)(2,1)} %fusion.64, bf16[1024,3072]{1,0:T(8,128)(2,1)S(1)} %bitcast.234, f32[1024,768]{1,0:T(8,128)S(1)} %copy-done.23), kind=kOutput, calls=%fused_computation.80 | convolution fusion | flops 4834983936 | bytes 14155776 | tf_op jit(solution)/shard_map/dot_general | solution.py:34
  427.7 5.0 fusion.100
  432.6 4.8 fusion.97
  437.4 141.5 %reduce-scatter.5.cloned.1.call-done = bf16[624,768]{1,0:T(8,128)(2,1)} async-done(((bf16[9984,768]{1,0:T(8,128)(2,1)}), bf16[624,768]{1,0:T(8,128)(2,1)}) %reduce-scatter.5.cloned.1.call-update) | async-done | bytes 958480 | tf_op jit(solution)/shard_map/reduce_scatter | solution.py:321
  581.6 6.3 add_convert_fusion.1
  588.0 47.8 %reduce-scatter.7.cloned.1.call-done = bf16[48,16]{1,0:T(8,128)(2,1)} async-done(((bf16[768,16]{1,0:T(8,128)(2,1)}), bf16[48,16]{1,0:T(8,128)(2,1)}) %reduce-scatter.7.cloned.1.call-update) | async-done | bytes 1552
  636.6 4.9 psum.38
  642.2 33.0 %all-reduce.3.cloned.1.call-done = bf16[624,768]{1,0:T(8,128)(2,1)} async-done(((bf16[624,768]{1,0:T(8,128)(2,1)}), bf16[624,768]{1,0:T(8,128)(2,1)}) %all-reduce.3.cloned.1.call-update) | async-done | bytes 958480 | tf_op jit(solution)/shard_map/psum | solution.py:329
  675.1 7.2 %fusion.133 = (bf16[624,768]{1,0:T(8,128)(2,1)}, f32[624,768]{1,0:T(8,128)}, f32[624,768]{1,0:T(8,128)}, f32[624,768]{1,0:T(8,128)}) fusion(f32[624,768]{1,0:T(8,128)} %param.25, f32[624]{0:T(1024)S(1)} %select_select_fusion, bf16[624,768]{1,0:T(8,128)(2,1)} %all-reduce.3.cloned.1.call-done, f32[624,768]{1,0:T(8,128)} %param.26, f32[624,768]{1,0:T(8,128)} %param.27), kind=kLoop, calls=%fused_computation.217 | loop fusion | flops 8146944 | bytes 13420992 | tf_op jit(solution)/shard_map/convert_element_type | solution.py:353
  (313 shorter events, 139.8 us)
Async XLA Ops:
  7.2 27.3 %copy-start.68 = (s32[2]{0:T(128)S(1)}, s32[2]{0:T(128)}, u32[]{:S(2)}) copy-start(s32[2]{0:T(128)} %param.24) | copy-start | bytes 28
  7.2 27.8 %copy-start.30 = (bf16[2,512,768]{2,1,0:T(8,128)(2,1)S(1)}, bf16[2,512,768]{2,1,0:T(8,128)(2,1)}, u32[]{:S(2)}) copy-start(bf16[2,512,768]{2,1,0:T(8,128)(2,1)} %param.21) | copy-start | bytes 4718596
  7.2 124.4 %all-gather.3.cloned.1.call-start = ((), (), s32[]{:S(2)}) async-start(), calls=%async_computation.2 | async-start | bytes 16293888 | tf_op jit(solution)/shard_map/all_gather | solution.py:179
  10.0 569.0 %reduce-scatter.5.cloned.1.call-start = ((), (), s32[]{:S(2)}) async-start(), calls=%async_computation.3 | async-start | bytes 16293888 | tf_op jit(solution)/shard_map/reduce_scatter | solution.py:321
  33.8 97.8 %copy-start.34 = (bf16[768,16]{0,1:T(8,128)(2,1)}, bf16[768,16]{0,1:T(8,128)(2,1)S(1)}, u32[]{:S(2)}) copy-start(bf16[768,16]{0,1:T(8,128)(2,1)S(1)} %reshape.228) | copy-start | bytes 73732
  34.5 189.3 %copy-start.59 = (f32[768]{0:T(1024)}, f32[768]{0:T(1024)S(1)}, u32[]{:S(2)}) copy-start(f32[768]{0:T(1024)S(1)} %get-tuple-element.220) | copy-start | bytes 9220
  34.5 288.7 %copy-start.42 = (f32[768]{0:T(1024)}, f32[768]{0:T(1024)S(1)}, u32[]{:S(2)}) copy-start(f32[768]{0:T(1024)S(1)} %get-tuple-element.221) | copy-start | bytes 9220
  186.5 37.3 %copy-start.13 = (f32[1024,768]{1,0:T(8,128)}, f32[1024,768]{1,0:T(8,128)S(1)}, u32[]{:S(2)}) copy-start(f32[1024,768]{1,0:T(8,128)S(1)} %get-tuple-element.291) | copy-start | bytes 9437188
  186.6 136.7 %copy-start.36 = (f32[1024]{0:T(1024)}, f32[1024]{0:T(1024)S(1)}, u32[]{:S(2)}) copy-start(f32[1024]{0:T(1024)S(1)} %broadcast_multiply_fusion.5) | copy-start | bytes 12292
  187.1 136.2 %copy-start.44 = (f32[1024]{0:T(1024)}, f32[1024]{0:T(1024)S(1)}, u32[]{:S(2)}) copy-start(f32[1024]{0:T(1024)S(1)} %add_rsqrt_fusion.1) | copy-start | bytes 12292
  187.1 36.8 %copy-start.61 = (f32[768]{0:T(1024)S(1)}, f32[768]{0:T(1024)}, u32[]{:S(2)}) copy-start(f32[768]{0:T(1024)} %get-tuple-element.219) | copy-start | bytes 9220
  236.2 47.9 %copy-start.40 = (bf16[2,1,768]{2,1,0:T(2,128)(2,1)}, bf16[2,1,768]{2,1,0:T(2,128)(2,1)S(1)}, u32[]{:S(2)}) copy-start(bf16[2,1,768]{2,1,0:T(2,128)(2,1)S(1)} %slice.126) | copy-start | bytes 9220
  237.8 46.4 %copy-start.56 = (f32[2,768]{1,0:T(2,128)}, f32[2,768]{1,0:T(2,128)S(1)}, u32[]{:S(2)}) copy-start(f32[2,768]{1,0:T(2,128)S(1)} %fusion.91) | copy-start | bytes 18436
  239.0 45.2 %copy-start.66 = (f32[2,3]{1,0:T(2,128)}, f32[2,3]{1,0:T(2,128)S(1)}, u32[]{:S(2)}) copy-start(f32[2,3]{1,0:T(2,128)S(1)} %get-tuple-element.282) | copy-start | bytes 76
  423.6 212.2 %reduce-scatter.7.cloned.1.call-start = ((), (), s32[]{:S(2)}) async-start(), calls=%async_computation.5 | async-start | bytes 208896
  427.6 247.5 %all-reduce.3.cloned.1.call-start = ((), (), s32[]{:S(2)}) async-start(), calls=%async_computation.4 | async-start | bytes 1916928 | tf_op jit(solution)/shard_map/psum | solution.py:329
  432.6 146.4 %copy-start.71 = (f32[3]{0:T(128)S(1)}, f32[3]{0:T(128)}, u32[]{:S(2)}) copy-start(f32[3]{0:T(128)} %param.31) | copy-start | bytes 40
  432.6 146.4 %copy-start.72 = (f32[3]{0:T(128)S(1)}, f32[3]{0:T(128)}, u32[]{:S(2)}) copy-start(f32[3]{0:T(128)} %param.32) | copy-start | bytes 40
  432.6 146.4 %copy-start.73 = (f32[3]{0:T(128)S(1)}, f32[3]{0:T(128)}, u32[]{:S(2)}) copy-start(f32[3]{0:T(128)} %param.33) | copy-start | bytes 40
  432.6 146.4 %copy-start.74 = (f32[3]{0:T(128)S(1)}, f32[3]{0:T(128)}, u32[]{:S(2)}) copy-start(f32[3]{0:T(128)} %get-tuple-element.265) | copy-start | bytes 40
  432.6 149.0 %copy-start.18 = (f32[1024,768]{1,0:T(8,128)S(1)}, f32[1024,768]{1,0:T(8,128)}, u32[]{:S(2)}) copy-start(f32[1024,768]{1,0:T(8,128)} %copy-done.16) | copy-start | bytes 9437188
  581.6 59.9 %copy-start.39 = (f32[16,48]{1,0:T(8,128)S(1)}, f32[16,48]{1,0:T(8,128)}, u32[]{:S(2)}) copy-start(f32[16,48]{1,0:T(8,128)} %param.28) | copy-start | bytes 9220
  581.6 59.9 %copy-start.54 = (f32[16,48]{1,0:T(8,128)S(1)}, f32[16,48]{1,0:T(8,128)}, u32[]{:S(2)}) copy-start(f32[16,48]{1,0:T(8,128)} %param.29) | copy-start | bytes 9220
  581.6 59.9 %copy-start.55 = (f32[16,48]{1,0:T(8,128)S(1)}, f32[16,48]{1,0:T(8,128)}, u32[]{:S(2)}) copy-start(f32[16,48]{1,0:T(8,128)} %param.30) | copy-start | bytes 9220
  (74 other events, 265.2 us)
Sparse Core Ops, SparseCore 0:
  10.9 120.6 all-gather.2
  423.6 155.3 reduce-scatter.4
  583.1 52.7 reduce-scatter.6
  638.0 37.0 all-reduce.2
where the time goes:
time: 698 us; the launch traced here: 690 us
  waiting for transfers between devices  316 us (45%)
  matrix products  188 us (27%)
  blocking collectives  67.7 us (10%)
  other arithmetic  51.2 us (7%)
  local copies, waits for them, and re-layouts  48.4 us (7%)
  between operations  17.7 us (3%)
    reduce_scatter x1, waiting for transfers between devices, on_device(): lax.psum_scatter(mat_grad.astype(jnp.bfloat16), 'fsdp', scatter_dimension...  142 us
    all_gather x1, waiting for transfers between devices, on_device(): lax.all_gather(mat_low, 'fsdp', axis=0, tiled=True)  93.3 us
    dot_general x8, matrix products, product_last(): lax.dot_general(first_arg, second_arg, (((1,), (1,)), ((), ())), preferre...  77.4 us
    unnamed x5, waiting for transfers between devices  47.9 us
    psum x1, blocking collectives, on_device(): lax.psum((ce_sum, jnp.sum(active), error_sum), ('dp', 'fsdp'))  39.1 us
    dot_general x8, matrix products, product(): return jnp.dot(first_arg, second_arg, preferred_element_type=jnp.float32)  36.4 us
    psum x1, waiting for transfers between devices, on_device(): lax.psum(mat_part.astype(jnp.bfloat16), 'dp').astype(jnp.float32)  33 us
    dot_general x8, matrix products, product_first(): lax.dot_general(first_arg, second_arg, (((0,), (0,)), ((), ())), preferre...  27.4 us
  transfers between devices with their start and end apart: 4, of which 4 were waited for; matrix products, arithmetic and copies ran while one was open for 4% of the time, Pallas kernels for 0%

commit v1 on v0

--- a/solution.py
+++ b/solution.py
@@ -18,6 +18,23 @@
 LN_EPS = 1e-12
 VEC_RATE = 0.5
 MASK_FILL = -1000000000.0
+
+
+def tell_panels(field_in, a_name, dim_at):
+    parts_n = lax.axis_size(a_name)
+    shelf = [(b, (b + 1) % parts_n) for b in range(parts_n)]
+    sides = [(b, (b - 1) % parts_n) for b in range(parts_n)]
+    u_next, a_next = ([field_in], [field_in])
+    for _ in range(parts_n // 2):
+        res = lax.ppermute(u_next[-1], a_name, perm=shelf)
+        u_next.append(res)
+    for _ in range((parts_n - 1) // 2):
+        a_next.append(lax.ppermute(a_next[-1], a_name, sides))
+    base_arr = jnp.concatenate([*u_next[::-1], *a_next[1:]], dim_at)
+    spare = jnp.roll(
+        base_arr, (lax.axis_index(a_name) - parts_n // 2) * field_in.shape[dim_at], dim_at
+    )
+    return spare
 
 
 def product(first_arg, second_arg):
@@ -177,7 +194,7 @@
     vec_low = vec_master.astype(jnp.bfloat16)
     matrices, vectors = (
         lax.all_gather(mat_low, "fsdp", axis=0, tiled=True),
-        lax.all_gather(vec_low, "fsdp", axis=1, tiled=True),
+        tell_panels(vec_low, "fsdp", 1),
     )
     w_query, w_key, w_value, w_out, w_pool, w_inner, w_outer = split_matrices(matrices)
     (

time: 698 us -> 741 us (1.062)
  matrix products: 188 us -> 230 us
  starting transfers between devices: 0.16 us -> 29.4 us
  waiting for transfers between devices: 316 us -> 290 us
    all_gather x1, waiting for transfers between devices: 93.3 us -> 56.9 us  [on_device(): lax.all_gather(mat_low, 'fsdp', axis=0, tiled=True)]
    ppermute x0 -> x15, starting transfers between devices: none -> 29 us  [the longest x7 28.4 us: tell_panels(): a_next.append(lax.ppermute(a_next[-1], a_name, sides))]
    dot_general x8, matrix products: 36.4 us -> 65 us  [product(): return jnp.dot(first_arg, second_arg, preferred_element_type=jnp.float32)]
    dot_general x8, matrix products: 27.4 us -> 41.9 us  [product_first(): lax.dot_general(first_arg, second_arg, (((0,), (0,)), ((), ())), preferre...]
    ppermute x0 -> x15, waiting for transfers between devices: none -> 11.3 us  [the longest x8 7.16 us: tell_panels(): res = lax.ppermute(u_next[-1], a_name, perm=shelf)]
  transfers between devices with their start and end apart: 4 -> 19, of which waited for: 4 -> 12; matrix products, arithmetic and copies ran while one was open for 4% -> 4% of each run, Pallas kernels for 0% -> 0%
where the time goes in v1:
time: 741 us; the launch traced here: 733 us
  waiting for transfers between devices  290 us (39%)
  matrix products  230 us (31%)
  blocking collectives  62.4 us (8%)
  other arithmetic  51.6 us (7%)
  local copies, waits for them, and re-layouts  50.4 us (7%)
  starting transfers between devices  29.4 us (4%)
  between operations  17.9 us (2%)
    reduce_scatter x1, waiting for transfers between devices, on_device(): lax.psum_scatter(mat_grad.astype(jnp.bfloat16), 'fsdp', scatter_dimension...  141 us
    dot_general x8, matrix products, product_last(): lax.dot_general(first_arg, second_arg, (((1,), (1,)), ((), ())), preferre...  76.3 us
    dot_general x8, matrix products, product(): return jnp.dot(first_arg, second_arg, preferred_element_type=jnp.float32)  65 us
    all_gather x1, waiting for transfers between devices, on_device(): lax.all_gather(mat_low, 'fsdp', axis=0, tiled=True)  56.9 us
    unnamed x5, waiting for transfers between devices  48 us
    dot_general x8, matrix products, product_first(): lax.dot_general(first_arg, second_arg, (((0,), (0,)), ((), ())), preferre...  41.9 us
    psum x1, blocking collectives, on_device(): lax.psum((ce_sum, jnp.sum(active), error_sum), ('dp', 'fsdp'))  38.8 us
    psum x1, waiting for transfers between devices, on_device(): lax.psum(mat_part.astype(jnp.bfloat16), 'dp').astype(jnp.float32)  33 us
  transfers between devices with their start and end apart: 19, of which 12 were waited for; matrix products, arithmetic and copies ran while one was open for 4% of the time, Pallas kernels for 0%

profile of v1, /device:TPU:0, one launch (start us, length us, event | category | flops | bytes accessed | tf_op | source)
XLA Modules:
  0.0 732.9 jit_solution(4224035854852971348)
XLA Ops:
  10.5 5.0 collective-permute-start.8
  36.2 18.7 %all-gather = bf16[16,48,16]{1,2,0:T(8,128)(2,1)S(1)} all-gather(bf16[1,48,16]{1,2,0:T(8,128)(2,1)S(1)} %convert_bitcast_fusion), channel_id=1, replica_groups=mesh['dp'=2,'fsdp'=16] {'fsdp'}, dimensions={0}, use_global_device_ids=true | all-gather | bytes 26112 | tf_op jit(solution)/shard_map/all_gather | solution.py:245
  75.2 56.9 %all-gather.3.cloned.1.call-done = bf16[9984,768]{1,0:T(8,128)(2,1)} async-done(((bf16[624,768]{1,0:T(8,128)(2,1)}), bf16[9984,768]{1,0:T(8,128)(2,1)}) %all-gather.3.cloned.1.call-update) | async-done | bytes 15335440 | tf_op jit(solution)/shard_map/all_gather | solution.py:196
  155.9 22.9 %while.27 = (s32[]{:T(128)}, bf16[2,512,12,64]{1,3,2,0:T(8,128)(2,1)}, f32[2,12,512,1]{2,1,3,0:T(8,128)S(1)}, bf16[2,512,12,64]{1,3,2,0:T(8,128)(2,1)}, s32[2]{0...) while((s32[]{:T(128)}, ...), condition=%wide.region_3.4_spmd, body=%wide.region_0.3_spmd.sunk | while | flops 843442688 | bytes 47427716 | solution.py:220
  187.6 34.7 %fusion.60 = (f32[1024,3072]{1,0:T(8,128)}, f32[1024,3072]{1,0:T(8,128)S(1)}) fusion(f32[3072]{0:T(1024)S(1)} %add.278, bf16[9984,768]{1,0:T(8,128)(2,1)} %all-gather.3.cloned.1.call-done, f32[1024,768]{1,0:T(8,128)S(1)} %get-tuple-element.291, f32[768]{0:T(1024)S(1)} %get-tuple-element.222, f32[768]{0:T(1024)S(1)} %get-tuple-element.223, ...), kind=kOutput, calls=%fused_computation.67 | convolution fusion | flops 5033951232 | bytes 33056768 | tf_op jit(solution)/shard_map/dot_general | solution.py:45
  222.4 38.5 %fusion.186 = (f32[1024]{0:T(1024)S(1)}, f32[1024,768]{1,0:T(8,128)S(1)}) fusion(f32[768]{0:T(1024)S(1)} %copy-done.67, bf16[9984,768]{1,0:T(8,128)(2,1)} %all-gather.3.cloned.1.call-done, f32[1024,3072]{1,0:T(8,128)S(1)} %get-tuple-element.297, f32[3072]{0:T(1024)S(1)} %copy-done.53, f32[768]{0:T(1024)S(1)} %get-tuple-element.222, ...), kind=kOutput, calls=%fused_computation.275 | convolution fusion | flops 5044960256 | bytes 23626752 | tf_op jit(solution)/shard_map/dot_general | solution.py:41
  266.8 38.8 %all-reduce = (f32[]{:T(128)}, f32[]{:T(128)}, f32[3]{0:T(128)}) all-reduce(f32[]{:T(128)} %get-tuple-element.230, f32[]{:T(128)} %get-tuple-element.229, f32[3]{0:T(128)S(1)} %get-tuple-element.283), channel_id=1, replica_groups=mesh['dp'=2,'fsdp'=16] {'dp','fsdp'}, use_global_device_ids=true, to_apply=%region_11.12 | all-reduce | flops 5 | bytes 40 | tf_op jit(solution)/shard_map/psum | solution.py:240
  321.4 19.5 %fusion.189 = (bf16[3072]{0:T(1024)(128)(2,1)}, bf16[1024,3072]{1,0:T(8,128)(2,1)}) fusion(f32[1024,3072]{1,0:T(8,128)} %get-tuple-element.296, bf16[9984,768]{1,0:T(8,128)(2,1)} %all-gather.3.cloned.1.call-done, f32[1024,768]{1,0:T(8,128)} %get-tuple-element.276, f32[1024,3072]{1,0:T(8,128)} %copy-done.88, f32[3072]{0:T(1024)S(1)} %add.278), kind=kOutput, calls=%fused_computation.278 | convolution fusion | flops 4882953216 | bytes 39340032 | tf_op jit(solution)/shard_map/dot_general | solution.py:45
  340.8 10.5 %multiply_reduce_fusion.1 = (bf16[768]{0:T(1024)(128)(2,1)}, f32[1024]{0:T(1024)S(1)}, f32[1024]{0:T(1024)S(1)}, bf16[768]{0:T(1024)(128)(2,1)}, f32[1024,768]{1,0:T(8,128)S(1)}) fusion(f32[1024,768]{1,0:T(8,128)S(1)} %copy-done.14, f32[1024]{0:T(1024)S(1)} %add_rsqrt_fusion.1, f32[1024]{0:T(1024)S(1)} %broadcast_multiply_fusion.5, ...), kind=kOutput, calls=%fused_computation.115 | convolution fusion | flops 4839698432 | bytes 20469760 | tf_op jit(solution)/shard_map/dot_general | solution.py:41
  365.2 51.8 %while.28 = (s32[]{:T(128)}, bf16[2,512,12,64]{1,3,2,0:T(8,128)(2,1)}, bf16[2,512,12,64]{1,3,2,0:T(8,128)(2,1)}, bf16[2,512,12,64]{1,3,2,0:T(8,128)(2,1)}, bf16[...) while((s32[]{:T(128)}, ...), condition=%wide.region_18.19_spmd, body=%wide.region_16.18_spmd.sunk | while | flops 2062412288 | bytes 140180784 | solution.py:292
  368.4 7.3 multiply_reduce_fusion.9
  375.7 7.2 multiply_convert_fusion.10
  394.2 7.3 multiply_reduce_fusion.9
  401.6 7.2 multiply_convert_fusion.10
  436.7 8.0 %fusion.78 = bf16[9984,768]{1,0:T(8,128)(2,1)} fusion(bf16[9984,768]{1,0:T(8,128)(2,1)} %fusion.98, bf16[1024,3072]{1,0:T(8,128)(2,1)S(1)} %bitcast.229, f32[1024,768]{1,0:T(8,128)S(1)} %copy-done.15, f32[768]{0:T(1024)S(1)} %copy-done.64, f32[768]{0:T(1024)S(1)} %copy-done.66, f32[1024]{0:T(1024)S(1)} %copy-done.47, f32[1024]{0:T(1024)S(1)} %copy-done.40), kind=kOutput, calls=%fused_computation.103 | convolution fusion | flops 4838129664 | bytes 14170112 | tf_op jit(solution)/shard_map/dot_general | solution.py:51
  444.7 21.4 %fusion.80 = bf16[9984,768]{1,0:T(8,128)(2,1)} fusion(bf16[9984,768]{1,0:T(8,128)(2,1)} %fusion.78, f32[1024,3072]{1,0:T(8,128)} %get-tuple-element.296, f32[1024,3072]{1,0:T(8,128)} %copy-done.88, f32[3072]{0:T(1024)S(1)} %copy-done.52, f32[1024,768]{1,0:T(8,128)S(1)} %copy-done.23), kind=kOutput, calls=%fused_computation.105 | convolution fusion | flops 4847566848 | bytes 33042432 | tf_op jit(solution)/shard_map/dot_general | solution.py:51
  470.5 5.0 fusion.117
  475.6 4.8 fusion.114
  480.4 141.1 %reduce-scatter.5.cloned.1.call-done = bf16[624,768]{1,0:T(8,128)(2,1)} async-done(((bf16[9984,768]{1,0:T(8,128)(2,1)}), bf16[624,768]{1,0:T(8,128)(2,1)}) %reduce-scatter.5.cloned.1.call-update) | async-done | bytes 958480 | tf_op jit(solution)/shard_map/reduce_scatter | solution.py:338
  624.1 6.3 add_convert_fusion.1
  630.4 47.9 %reduce-scatter.7.cloned.1.call-done = bf16[48,16]{1,0:T(8,128)(2,1)} async-done(((bf16[768,16]{1,0:T(8,128)(2,1)}), bf16[48,16]{1,0:T(8,128)(2,1)}) %reduce-scatter.7.cloned.1.call-update) | async-done | bytes 1552
  679.1 4.9 psum.38
  684.7 33.0 %all-reduce.3.cloned.1.call-done = bf16[624,768]{1,0:T(8,128)(2,1)} async-done(((bf16[624,768]{1,0:T(8,128)(2,1)}), bf16[624,768]{1,0:T(8,128)(2,1)}) %all-reduce.3.cloned.1.call-update) | async-done | bytes 958480 | tf_op jit(solution)/shard_map/psum | solution.py:346
  717.7 7.2 fusion.181
  (356 shorter events, 182.8 us)
Async XLA Ops:
  7.2 124.8 %all-gather.3.cloned.1.call-start = ((), (), s32[]{:S(2)}) async-start(), calls=%async_computation.2 | async-start | bytes 16293888 | tf_op jit(solution)/shard_map/all_gather | solution.py:196
  9.9 611.5 %reduce-scatter.5.cloned.1.call-start = ((), (), s32[]{:S(2)}) async-start(), calls=%async_computation.3 | async-start | bytes 16293888 | tf_op jit(solution)/shard_map/reduce_scatter | solution.py:338
  10.0 6.8 collective-permute-start
  10.5 6.4 collective-permute-start.8
  16.8 5.7 collective-permute-start.1
  16.9 8.9 %collective-permute-start.9 = (bf16[16,48]{1,0:T(8,128)(2,1)S(1)}, bf16[16,48]{1,0:T(8,128)(2,1)S(1)}, u32[]{:S(2)}, u32[]{:S(2)}) collective-permute-start(bf16[16,48]{1,0:T(8,128)(2,1)S(1)} %collective-permute-done.8), channel_id=1, source_target_pairs={{0,15},{1,0},{2,1},{3,2},{4,3},{5,4},{6,5},{7,6},{8,7},{9,8},{10,9... | collective-permute-start | bytes 4616 | tf_op jit(solution)/shard_map/ppermute | solution.py:32
  22.5 7.8 %collective-permute-start.2 = (bf16[16,48]{1,0:T(8,128)(2,1)S(1)}, bf16[16,48]{1,0:T(8,128)(2,1)S(1)}, u32[]{:S(2)}, u32[]{:S(2)}) collective-permute-start(bf16[16,48]{1,0:T(8,128)(2,1)S(1)} %collective-permute-done.1), channel_id=1, source_target_pairs={{0,1},{1,2},{2,3},{3,4},{4,5},{5,6},{6,7},{7,8},{8,9},{9,10},{10,1... | collective-permute-start | bytes 4616 | tf_op jit(solution)/shard_map/ppermute | solution.py:29
  25.8 5.8 collective-permute-start.10
  30.3 5.9 collective-permute-start.3
  31.6 23.5 %collective-permute-start.11 = (bf16[16,48]{1,0:T(8,128)(2,1)S(1)}, bf16[16,48]{1,0:T(8,128)(2,1)S(1)}, u32[]{:S(2)}, u32[]{:S(2)}) collective-permute-start(bf16[16,48]{1,0:T(8,128)(2,1)S(1)} %collective-permute-done.10), channel_id=1, source_target_pairs={{0,15},{1,0},{2,1},{3,2},{4,3},{5,4},{6,5},{7,6},{8,7},{9,8},{10,9... | collective-permute-start | bytes 4616 | tf_op jit(solution)/shard_map/ppermute | solution.py:32
  36.2 19.9 %collective-permute-start.4 = (bf16[16,48]{1,0:T(8,128)(2,1)S(1)}, bf16[16,48]{1,0:T(8,128)(2,1)S(1)}, u32[]{:S(2)}, u32[]{:S(2)}) collective-permute-start(bf16[16,48]{1,0:T(8,128)(2,1)S(1)} %collective-permute-done.3), channel_id=1, source_target_pairs={{0,1},{1,2},{2,3},{3,4},{4,5},{5,6},{6,7},{7,8},{8,9},{9,10},{10,1... | collective-permute-start | bytes 4616 | tf_op jit(solution)/shard_map/ppermute | solution.py:29
  55.0 2.3 collective-permute-start.12
  56.1 5.7 collective-permute-start.5
  57.4 5.7 collective-permute-start.13
  61.8 5.9 collective-permute-start.6
  63.1 5.9 collective-permute-start.14
  67.7 5.9 collective-permute-start.7
  68.4 253.0 %copy-start.51 = (f32[3072]{0:T(1024)}, f32[3072]{0:T(1024)S(1)}, u32[]{:S(2)}) copy-start(f32[3072]{0:T(1024)S(1)} %add.278) | copy-start | bytes 36868
  75.2 147.2 %copy-start.65 = (f32[768]{0:T(1024)}, f32[768]{0:T(1024)S(1)}, u32[]{:S(2)}) copy-start(f32[768]{0:T(1024)S(1)} %get-tuple-element.223) | copy-start | bytes 9220
  187.1 164.2 %copy-start.39 = (f32[1024]{0:T(1024)}, f32[1024]{0:T(1024)S(1)}, u32[]{:S(2)}) copy-start(f32[1024]{0:T(1024)S(1)} %broadcast_multiply_fusion.5) | copy-start | bytes 12292
  187.6 163.7 %copy-start.46 = (f32[1024]{0:T(1024)}, f32[1024]{0:T(1024)S(1)}, u32[]{:S(2)}) copy-start(f32[1024]{0:T(1024)S(1)} %add_rsqrt_fusion.1) | copy-start | bytes 12292
  466.2 212.1 %reduce-scatter.7.cloned.1.call-start = ((), (), s32[]{:S(2)}) async-start(), calls=%async_computation.5 | async-start | bytes 208896
  470.2 247.4 %all-reduce.3.cloned.1.call-start = ((), (), s32[]{:S(2)}) async-start(), calls=%async_computation.4 | async-start | bytes 1916928 | tf_op jit(solution)/shard_map/psum | solution.py:346
  475.6 148.5 %copy-start.18 = (f32[1024,768]{1,0:T(8,128)S(1)}, f32[1024,768]{1,0:T(8,128)}, u32[]{:S(2)}) copy-start(f32[1024,768]{1,0:T(8,128)} %copy-done.16) | copy-start | bytes 9437188
  (93 other events, 1643.4 us)
Sparse Core Ops, SparseCore 0:
  10.9 121.0 all-gather.2
  466.2 155.1 reduce-scatter.4
  625.6 52.7 reduce-scatter.6
  680.5 37.1 all-reduce.2
